TPU v7x, 256 devices: a whole 4x4x8 slice. The times are simulated.
256 devices in a mesh: row: 8 (over z), col: 32 (over x, y, core).
Axes of the slice: x: 4, y: 4, z: 8, core: 2. Of those that a mesh axis runs over, the one named last changes fastest.
Arguments:
- three_index: float32 [256, 512, 1024], P('col', None, 'row'), may hold values from -1.2 to 1.2
- occ_energy: float32 [256], replicated, may hold values from -2 to -0.5
- vir_energy: float32 [512], replicated, may hold values from 0.5 to 3
- block_mask: int32 [256, 8, 16], replicated, may hold values from 0 to 1, as said below
- pair_list: int32 [256, 4], P('col'), may hold values from -1 to 3, as said below
Outputs:
- response_density: float32 [256, 512, 1024], P('col', None, 'row')
- virtual_density: float32 [512, 512], replicated
Inputs may be any that keep to these rules, and one draw needn't show every extreme that they name: `block_mask`: each orbital keeps between 32 and 64 of its 128 blocks; some orbital keeps exactly 64. `pair_list`: in each row the live entries come first and are distinct, then -1; every orbital lists at least one partner class; some orbital lists 4.
All inputs are finite; a program needn't handle non-finite values.
Results may differ from a plain program's by a relative error of at most 0.0003.
Values sent between devices are 32-bit elements; how exact they have to be, the bound alone decides.
A program may use at most 128 MiB of HBM per device.

v0:
```python
import jax
import jax.numpy as jnp
from jax import lax
from jax.sharding import PartitionSpec as P

NVIR = 512
NAUX = 1024
BLOCK = 64
STEPS = 2
PAIRS_DEV = 4


def spread(block, axis, holder):
    block = jnp.where(lax.axis_index(axis) == holder, block, jnp.zeros_like(block))
    return lax.psum(block, axis)


def expand_mask(block_rows):
    widened = jnp.repeat(block_rows.astype(jnp.float32), BLOCK, axis=-2)
    return jnp.repeat(widened, BLOCK, axis=-1)


def pair_terms(own_rows, partner, energy_own, energy_partner, virtual):
    cross_term = lax.dot_general(
        own_rows,
        partner,
        (((1,), (1,)), ((), ())),
        precision=lax.Precision.HIGHEST,
        preferred_element_type=jnp.float32,
    )
    denominator = energy_own + energy_partner - virtual[:, None] - virtual[None, :]
    amplitude = cross_term / denominator
    weighted = 2.0 * amplitude - amplitude.T
    response = jnp.dot(
        weighted, partner, precision=lax.Precision.HIGHEST, preferred_element_type=jnp.float32
    )
    virt_density = lax.dot_general(
        weighted,
        amplitude,
        (((1,), (1,)), ((), ())),
        precision=lax.Precision.HIGHEST,
        preferred_element_type=jnp.float32,
    )
    return (response, virt_density)


def on_device(three_index, occ_energy, vir_energy, block_mask, pair_list):
    row_index = lax.axis_index("row")
    col_index = lax.axis_index("col")
    row_count = lax.axis_size("row")
    col_count = lax.axis_size("col")
    own_orbital = col_index * row_count + row_index
    gathered = lax.all_to_all(three_index, "row", split_axis=0, concat_axis=2, tiled=True)
    own_rows = gathered[0] * expand_mask(block_mask[own_orbital])
    panels = []
    for owner_step in range(STEPS):
        first_root = 2 * owner_step
        second_root = first_root + 1
        panels.append(spread(own_rows, "col", first_root))
        panels.append(spread(own_rows, "col", second_root))
    stacked = jnp.stack(panels)
    energy_own = occ_energy[own_orbital]
    response_sum = jnp.zeros((NVIR, NAUX), jnp.float32)
    density_sum = jnp.zeros((NVIR, NVIR), jnp.float32)
    for slot_index in range(PAIRS_DEV):
        listed = pair_list[row_index, slot_index]
        panel_index = jnp.maximum(listed, 0)
        partner = stacked[panel_index]
        energy_partner = occ_energy[panel_index * row_count + row_index]
        live = (listed >= 0).astype(jnp.float32)
        response, virt_density = pair_terms(
            own_rows, partner, energy_own, energy_partner, vir_energy
        )
        response = live * response
        virt_density = live * virt_density
        response_sum = response_sum + response
        density_sum = density_sum + virt_density
    returned = lax.all_to_all(response_sum[None], "row", split_axis=2, concat_axis=0, tiled=True)
    total = lax.psum(density_sum, ("row", "col"))
    return (returned, total / (row_count * col_count))


def solution(mesh):
    placed = (P("col", None, "row"), P(), P(), P(), P("col", None))
    return jax.shard_map(
        on_device,
        mesh=mesh,
        in_specs=placed,
        out_specs=(P("col", None, "row"), P()),
        check_vma=False,
    )
```

profile of v0, /device:TPU:2, one launch (start us, length us, event | category | flops | bytes accessed | tf_op | source)
XLA Modules:
  0.0 567.0 jit_solution(334607822717897980)
XLA Ops:
  7.2 2.9 copy.21
  10.1 8.5 %all-to-all-start = ((f32[8,512,128]{1,2,0:T(8,128)}), f32[8,512,128]{1,2,0:T(8,128)S(1)}, u32[]{:S(2)}, u32[]{:S(2)}) async-start(f32[8,512,128]{1,2,0:T(8,128)} %copy.21), calls=%async_computation | async-start | bytes 4194304 | tf_op jit(solution)/shard_map/all_to_all | solution.py:53
  19.1 50.7 %all-to-all-done = f32[8,512,128]{1,2,0:T(8,128)S(1)} async-done(((f32[8,512,128]{1,2,0:T(8,128)}), f32[8,512,128]{1,2,0:T(8,128)S(1)}, u32[]{:S(2)}, u32[]{:S(2)}) %all-to-all-start) | async-done | bytes 2097184 | tf_op jit(solution)/shard_map/all_to_all | solution.py:53
  69.8 3.9 select_bitcast_fusion
  86.0 2.2 bitcast_multiply_fusion.1
  88.2 111.9 %all-reduce.6.cloned.1.call-done = (f32[1,512,1024]{1,2,0:T(8,128)}, f32[1,512,1024]{1,2,0:T(8,128)}, f32[1,512,1024]{1,2,0:T(8,128)}, f32[1,512,1024]{1,2,0:T(8,128)}) async-done(((f32[1,512,1024]{1,2,0:T(8,128)}, f32[1,512,1024]{1,2,0:T(8,128)}, f32[1,512,1024]{1,2,0:T(8,128)}, f32[1,512,1024]{1,2,0:T(8,128)}), (f32[1,512,1024]{1,2,0:T(8,128)}, f32[1,512,1024]{1,2,0:T(8,128)}, f32[1,512,1024]{1,2,0:T(8,128)}, ...) | async-done | bytes 8388624 | tf_op jit(solution)/shard_map/psum | solution.py:15
  205.8 3.5 fusion.2
  209.3 4.6 fusion.6
  213.9 4.9 fusion.10
  218.7 4.5 fusion.14
  223.3 2.7 copy.24
  229.9 9.2 %fusion.8 = f32[512,1024]{1,0:T(8,128)S(1)} fusion(f32[4,512,1024]{1,2,0:T(8,128)} %copy-done.2, s32[]{:T(128)} %bitcast.18, f32[512,512]{1,0:T(8,128)S(1)} %copy-done.5, f32[512]{0:T(512)S(1)} %get-tuple-element.11, f32[512]{0:T(512)S(1)} %copy-done.19, f32[512,512]{0,1:T(8,128)} %copy.25), kind=kOutput, calls=%fused_computation.9 | convolution fusion | flops 3222798336 | bytes 6300160 | tf_op jit(solution)/shard_map/dot_general | solution.py:34
  239.1 8.7 %fusion.4 = f32[512,1024]{1,0:T(8,128)S(1)} fusion(f32[4,512,1024]{1,2,0:T(8,128)} %copy-done.2, s32[]{:T(128)} %bitcast.23, f32[512,512]{1,0:T(8,128)S(1)} %copy-done.3, f32[512]{0:T(512)S(1)} %get-tuple-element.13, f32[512]{0:T(512)S(1)} %copy-done.19, f32[512,512]{0,1:T(8,128)S(1)} %copy-done.13), kind=kOutput, calls=%fused_computation.5 | convolution fusion | flops 3222798336 | bytes 6300160 | tf_op jit(solution)/shard_map/dot_general | solution.py:34
  247.9 7.2 %fusion = f32[512,1024]{1,0:T(8,128)S(1)} fusion(f32[4,512,1024]{1,2,0:T(8,128)S(1)} %bitcast.112, s32[]{:T(128)} %bitcast.28, f32[512,512]{1,0:T(8,128)S(1)} %fusion.2, f32[512]{0:T(512)S(1)} %get-tuple-element.12, f32[512]{0:T(512)S(1)} %copy-done.19, f32[512,512]{0,1:T(8,128)S(1)} %copy-done.11), kind=kOutput, calls=%fused_computation.1 | convolution fusion | flops 3222798336 | bytes 6299652 | tf_op jit(solution)/shard_map/dot_general | solution.py:34
  255.1 7.2 %add_bitcast_fusion = f32[1,512,1024]{2,1,0:T(8,128)S(1)} fusion(f32[512,1024]{1,0:T(8,128)S(1)} %fusion, f32[512,1024]{1,0:T(8,128)S(1)} %fusion.4, f32[512,1024]{1,0:T(8,128)S(1)} %fusion.8, f32[4,512,1024]{1,2,0:T(8,128)S(1)} %bitcast.112, s32[]{:T(128)} %bitcast.13, f32[]{:T(128)} %bitcast.27, f32[]{:T(128)} %bitcast.22, f32[]{:T(128)} %bitcast.17, ...), kind=kOutput, calls=%fused_computation.18 | convolution fusion | flops 3226468352 | bytes 12591124 | tf_op jit(solution)/shard_map/dot_general | solution.py:34
  262.3 3.7 copy.28
  266.0 7.0 %all-to-all-start.1 = ((f32[1,512,1024]{1,0,2:T(1,128)}), f32[1,512,1024]{1,0,2:T(1,128)S(1)}, u32[]{:S(2)}, u32[]{:S(2)}) async-start(f32[1,512,1024]{1,0,2:T(1,128)} %copy.28), calls=%async_computation.1 | async-start | bytes 4194304 | tf_op jit(solution)/shard_map/all_to_all | solution.py:78
  273.3 4.5 convolution_multiply_fusion.3
  277.8 2.5 fusion.28
  280.4 2.5 fusion.27
  282.9 3.5 fusion.26
  286.4 267.5 %all-reduce.4.cloned.1.call-done = f32[512,512]{1,0:T(8,128)} async-done(((f32[512,512]{1,0:T(8,128)}), f32[512,512]{1,0:T(8,128)}) %all-reduce.4.cloned.1.call-update) | async-done | bytes 1048592 | tf_op jit(solution)/shard_map/psum | solution.py:79
  553.9 2.3 broadcast_multiply_fusion
  556.2 3.6 copy.29
  (67 shorter events, 12.7 us)
Async XLA Ops:
  7.2 11.5 %copy-start = (s32[256,8,16]{0,2,1:T(8,128)S(1)}, s32[256,8,16]{0,2,1:T(8,128)}, u32[]{:S(2)}) copy-start(s32[256,8,16]{0,2,1:T(8,128)} %param.8) | copy-start | bytes 393220
  10.1 59.7 %all-to-all-start = ((f32[8,512,128]{1,2,0:T(8,128)}), f32[8,512,128]{1,2,0:T(8,128)S(1)}, u32[]{:S(2)}, u32[]{:S(2)}) async-start(f32[8,512,128]{1,2,0:T(8,128)} %copy.21), calls=%async_computation | async-start | bytes 4194304 | tf_op jit(solution)/shard_map/all_to_all | solution.py:53
  18.6 181.6 %all-reduce.6.cloned.1.call-start = ((), (), s32[]{:S(2)}) async-start(), calls=%async_computation.3 | async-start | bytes 16777216 | tf_op jit(solution)/shard_map/psum | solution.py:15
  69.8 4.0 copy-start.1
  73.7 6.4 %copy-start.17 = (f32[256]{0:T(256)S(1)}, f32[256]{0:T(256)}, u32[]{:S(2)}) copy-start(f32[256]{0:T(256)} %param.6) | copy-start | bytes 3076
  73.7 12.0 %copy-start.19 = (f32[512]{0:T(512)S(1)}, f32[512]{0:T(512)}, u32[]{:S(2)}) copy-start(f32[512]{0:T(512)} %param.7) | copy-start | bytes 6148
  200.2 2.2 copy-start.10
  202.4 1.6 copy-start.9
  205.8 13.0 %copy-start.2 = (f32[4,512,1024]{1,2,0:T(8,128)}, f32[4,512,1024]{1,2,0:T(8,128)S(1)}, u32[]{:S(2)}) copy-start(f32[4,512,1024]{1,2,0:T(8,128)S(1)} %constant_dynamic-update-slice_fusion) | copy-start | bytes 25165828
  223.2 2.7 copy-start.5
  223.2 4.0 copy-start.3
  229.9 9.2 %copy-start.13 = (f32[512,512]{0,1:T(8,128)S(1)}, f32[512,512]{0,1:T(8,128)}, u32[]{:S(2)}) copy-start(f32[512,512]{0,1:T(8,128)} %copy.26) | copy-start | bytes 3145732
  229.9 17.9 %slice-start = ((s8[8388608]{0:T(1024)(128)(4,1)}), s8[4194304]{0:T(1024)(128)(4,1)S(1)}, s32[]{:S(2)}) async-start(s8[8388608]{0:T(1024)(128)(4,1)} %bitcast.111), calls=%async_computation.4 | async-start | bytes 8388608
  239.1 8.7 %slice-start.1 = ((s8[8388608]{0:T(1024)(128)(4,1)}), s8[4194304]{0:T(1024)(128)(4,1)S(1)}, s32[]{:S(2)}) async-start(s8[8388608]{0:T(1024)(128)(4,1)} %bitcast.111), calls=%async_computation.5 | async-start | bytes 8388608
  239.1 8.7 %copy-start.11 = (f32[512,512]{0,1:T(8,128)S(1)}, f32[512,512]{0,1:T(8,128)}, u32[]{:S(2)}) copy-start(f32[512,512]{0,1:T(8,128)} %copy.27) | copy-start | bytes 3145732
  247.9 7.2 %copy-start.7 = (f32[512,512]{1,0:T(8,128)S(1)}, f32[512,512]{1,0:T(8,128)}, u32[]{:S(2)}) copy-start(f32[512,512]{1,0:T(8,128)} %fusion.14) | copy-start | bytes 3145732
  247.9 7.2 %copy-start.16 = (f32[512,512]{0,1:T(8,128)S(1)}, f32[512,512]{0,1:T(8,128)}, u32[]{:S(2)}) copy-start(f32[512,512]{0,1:T(8,128)} %copy.24) | copy-start | bytes 3145732
  266.0 290.2 %all-to-all-start.1 = ((f32[1,512,1024]{1,0,2:T(1,128)}), f32[1,512,1024]{1,0,2:T(1,128)S(1)}, u32[]{:S(2)}, u32[]{:S(2)}) async-start(f32[1,512,1024]{1,0,2:T(1,128)} %copy.28), calls=%async_computation.1 | async-start | bytes 4194304 | tf_op jit(solution)/shard_map/all_to_all | solution.py:78
  273.0 280.9 %all-reduce.4.cloned.1.call-start = ((), (), s32[]{:S(2)}) async-start(), calls=%async_computation.2 | async-start | bytes 2097152 | tf_op jit(solution)/shard_map/psum | solution.py:79
  273.3 4.5 copy-start.6
  273.3 4.5 copy-start.15
  277.8 2.5 copy-start.4
  277.8 2.5 copy-start.14
  280.3 2.5 copy-start.12
  (2 other events, 2.3 us)
Sparse Core Ops, SparseCore 0:
  73.9 126.2 all-reduce.5
  286.5 267.3 all-reduce.3
where the time goes:
time: 576 us; the launch traced here: 567 us
  waiting for transfers between devices  430 us (75%)
  matrix products  62.6 us (11%)
  local copies, waits for them, and re-layouts  25.2 us (4%)
  between operations  24.9 us (4%)
  starting transfers between devices  15.8 us (3%)
  other arithmetic  8.42 us (1%)
    psum x1, waiting for transfers between devices, on_device(): total = lax.psum(density_sum, ('row', 'col'))  267 us
    psum x1, waiting for transfers between devices, spread(): return lax.psum(block, axis)  112 us
    all_to_all x1, waiting for transfers between devices, on_device(): lax.all_to_all(three_index, 'row', split_axis=0, concat_axis=2, tiled=True)  50.7 us
    dot_general x4, matrix products, pair_terms(): jnp.dot(weighted, partner, precision=lax.Precision.HIGHEST, preferred_ele...  32.2 us
    dot_general x4, matrix products, pair_terms(): lax.dot_general(own_rows, partner, (((1,), (1,)), ((), ())), precision=la...  17.5 us
    dot_general x4, matrix products, pair_terms(): lax.dot_general(weighted, amplitude, (((1,), (1,)), ((), ())), precision=...  12.9 us
  transfers between devices with their start and end apart: 4, of which 3 were waited for; matrix products, arithmetic and copies ran while one was open for 3% of the time, Pallas kernels for 0%

commit v1 on v0

--- a/solution.py
+++ b/solution.py
@@ -76,7 +76,7 @@
         response_sum = response_sum + response
         density_sum = density_sum + virt_density
     returned = lax.all_to_all(response_sum[None], "row", split_axis=2, concat_axis=0, tiled=True)
-    total = lax.psum(density_sum, ("row", "col"))
+    total = lax.psum(lax.psum(density_sum, axis_name="row"), axis_name="col")
     return (returned, total / (row_count * col_count))
 
 

time: 576 us -> 514 us (0.89)
  the two profiles are of different devices: /device:TPU:2 before, /device:TPU:1 now
where the time goes in v1:
time: 514 us; the launch traced here: 505 us
  waiting for transfers between devices  368 us (72%)
  matrix products  62.6 us (12%)
  local copies, waits for them, and re-layouts  25.2 us (5%)
  between operations  24.6 us (5%)
  starting transfers between devices  16.1 us (3%)
  other arithmetic  8.42 us (2%)
    psum x2, waiting for transfers between devices, on_device(): total = lax.psum(lax.psum(density_sum, axis_name='row'), axis_name='col')  204 us
    psum x1, waiting for transfers between devices, spread(): return lax.psum(block, axis)  112 us
    all_to_all x1, waiting for transfers between devices, on_device(): lax.all_to_all(three_index, 'row', split_axis=0, concat_axis=2, tiled=True)  51.1 us
    dot_general x4, matrix products, pair_terms(): jnp.dot(weighted, partner, precision=lax.Precision.HIGHEST, preferred_ele...  32.2 us
    dot_general x4, matrix products, pair_terms(): lax.dot_general(own_rows, partner, (((1,), (1,)), ((), ())), precision=la...  17.5 us
    dot_general x4, matrix products, pair_terms(): lax.dot_general(weighted, amplitude, (((1,), (1,)), ((), ())), precision=...  12.9 us
  transfers between devices with their start and end apart: 5, of which 4 were waited for; matrix products, arithmetic and copies ran while one was open for 4% of the time, Pallas kernels for 0%

profile of v1, /device:TPU:1, one launch (start us, length us, event | category | flops | bytes accessed | tf_op | source)
XLA Modules:
  0.0 504.5 jit_solution(13505209922436045203)
XLA Ops:
  7.2 2.9 copy.21
  10.1 9.0 %all-to-all-start = ((f32[8,512,128]{1,2,0:T(8,128)}), f32[8,512,128]{1,2,0:T(8,128)S(1)}, u32[]{:S(2)}, u32[]{:S(2)}) async-start(f32[8,512,128]{1,2,0:T(8,128)} %copy.21), calls=%async_computation | async-start | bytes 4194304 | tf_op jit(solution)/shard_map/all_to_all | solution.py:53
  19.6 51.1 %all-to-all-done = f32[8,512,128]{1,2,0:T(8,128)S(1)} async-done(((f32[8,512,128]{1,2,0:T(8,128)}), f32[8,512,128]{1,2,0:T(8,128)S(1)}, u32[]{:S(2)}, u32[]{:S(2)}) %all-to-all-start) | async-done | bytes 2097184 | tf_op jit(solution)/shard_map/all_to_all | solution.py:53
  70.8 3.9 select_bitcast_fusion
  89.2 112.1 %all-reduce.9.cloned.1.call-done = (f32[1,512,1024]{1,2,0:T(8,128)}, f32[1,512,1024]{1,2,0:T(8,128)}, f32[1,512,1024]{1,2,0:T(8,128)}, f32[1,512,1024]{1,2,0:T(8,128)}) async-done(((f32[1,512,1024]{1,2,0:T(8,128)}, f32[1,512,1024]{1,2,0:T(8,128)}, f32[1,512,1024]{1,2,0:T(8,128)}, f32[1,512,1024]{1,2,0:T(8,128)}), (f32[1,512,1024]{1,2,0:T(8,128)}, f32[1,512,1024]{1,2,0:T(8,128)}, f32[1,512,1024]{1,2,0:T(8,128)}, ...) | async-done | bytes 8388624 | tf_op jit(solution)/shard_map/psum | solution.py:15
  206.9 3.5 fusion.2
  210.5 4.6 fusion.6
  215.0 4.9 fusion.10
  219.9 4.5 fusion.14
  224.4 2.7 copy.24
  231.1 9.2 %fusion.8 = f32[512,1024]{1,0:T(8,128)S(1)} fusion(f32[4,512,1024]{1,2,0:T(8,128)} %copy-done.2, s32[]{:T(128)} %bitcast.18, f32[512,512]{1,0:T(8,128)S(1)} %copy-done.5, f32[512]{0:T(512)S(1)} %get-tuple-element.11, f32[512]{0:T(512)S(1)} %copy-done.19, f32[512,512]{0,1:T(8,128)} %copy.25), kind=kOutput, calls=%fused_computation.9 | convolution fusion | flops 3222798336 | bytes 6300160 | tf_op jit(solution)/shard_map/dot_general | solution.py:34
  240.3 8.7 %fusion.4 = f32[512,1024]{1,0:T(8,128)S(1)} fusion(f32[4,512,1024]{1,2,0:T(8,128)} %copy-done.2, s32[]{:T(128)} %bitcast.23, f32[512,512]{1,0:T(8,128)S(1)} %copy-done.3, f32[512]{0:T(512)S(1)} %get-tuple-element.13, f32[512]{0:T(512)S(1)} %copy-done.19, f32[512,512]{0,1:T(8,128)S(1)} %copy-done.13), kind=kOutput, calls=%fused_computation.5 | convolution fusion | flops 3222798336 | bytes 6300160 | tf_op jit(solution)/shard_map/dot_general | solution.py:34
  249.1 7.2 %fusion = f32[512,1024]{1,0:T(8,128)S(1)} fusion(f32[4,512,1024]{1,2,0:T(8,128)S(1)} %bitcast.112, s32[]{:T(128)} %bitcast.28, f32[512,512]{1,0:T(8,128)S(1)} %fusion.2, f32[512]{0:T(512)S(1)} %get-tuple-element.12, f32[512]{0:T(512)S(1)} %copy-done.19, f32[512,512]{0,1:T(8,128)S(1)} %copy-done.11), kind=kOutput, calls=%fused_computation.1 | convolution fusion | flops 3222798336 | bytes 6299652 | tf_op jit(solution)/shard_map/dot_general | solution.py:34
  256.3 7.2 %add_bitcast_fusion = f32[1,512,1024]{2,1,0:T(8,128)S(1)} fusion(f32[512,1024]{1,0:T(8,128)S(1)} %fusion, f32[512,1024]{1,0:T(8,128)S(1)} %fusion.4, f32[512,1024]{1,0:T(8,128)S(1)} %fusion.8, f32[4,512,1024]{1,2,0:T(8,128)S(1)} %bitcast.112, s32[]{:T(128)} %bitcast.13, f32[]{:T(128)} %bitcast.27, f32[]{:T(128)} %bitcast.22, f32[]{:T(128)} %bitcast.17, ...), kind=kOutput, calls=%fused_computation.18 | convolution fusion | flops 3226468352 | bytes 12591124 | tf_op jit(solution)/shard_map/dot_general | solution.py:34
  263.5 3.7 copy.28
  267.2 6.7 %all-to-all-start.1 = ((f32[1,512,1024]{1,0,2:T(1,128)}), f32[1,512,1024]{1,0,2:T(1,128)S(1)}, u32[]{:S(2)}, u32[]{:S(2)}) async-start(f32[1,512,1024]{1,0,2:T(1,128)} %copy.28), calls=%async_computation.1 | async-start | bytes 4194304 | tf_op jit(solution)/shard_map/all_to_all | solution.py:78
  274.2 4.5 convolution_multiply_fusion.3
  278.7 2.5 fusion.28
  281.3 2.5 fusion.27
  283.8 3.5 fusion.26
  287.3 82.9 %all-reduce.5.cloned.1.call-done = f32[512,512]{1,0:T(8,128)} async-done(((f32[512,512]{1,0:T(8,128)}), f32[512,512]{1,0:T(8,128)}) %all-reduce.5.cloned.1.call-update) | async-done | bytes 1048592 | tf_op jit(solution)/shard_map/psum | solution.py:79
  370.3 121.4 %all-reduce.7.cloned.1.call-done = f32[512,512]{1,0:T(8,128)} async-done(((f32[512,512]{1,0:T(8,128)}), f32[512,512]{1,0:T(8,128)}) %all-reduce.7.cloned.1.call-update) | async-done | bytes 1048592 | tf_op jit(solution)/shard_map/psum | solution.py:79
  491.7 2.3 broadcast_multiply_fusion
  494.0 3.6 copy.29
  (70 shorter events, 14.9 us)
Async XLA Ops:
  7.2 12.0 %copy-start = (s32[256,8,16]{0,2,1:T(8,128)S(1)}, s32[256,8,16]{0,2,1:T(8,128)}, u32[]{:S(2)}) copy-start(s32[256,8,16]{0,2,1:T(8,128)} %param.8) | copy-start | bytes 393220
  10.1 60.7 %all-to-all-start = ((f32[8,512,128]{1,2,0:T(8,128)}), f32[8,512,128]{1,2,0:T(8,128)S(1)}, u32[]{:S(2)}, u32[]{:S(2)}) async-start(f32[8,512,128]{1,2,0:T(8,128)} %copy.21), calls=%async_computation | async-start | bytes 4194304 | tf_op jit(solution)/shard_map/all_to_all | solution.py:53
  19.1 182.3 %all-reduce.9.cloned.1.call-start = ((), (), s32[]{:S(2)}) async-start(), calls=%async_computation.4 | async-start | bytes 16777216 | tf_op jit(solution)/shard_map/psum | solution.py:15
  70.8 4.0 copy-start.1
  74.7 6.4 %copy-start.17 = (f32[256]{0:T(256)S(1)}, f32[256]{0:T(256)}, u32[]{:S(2)}) copy-start(f32[256]{0:T(256)} %param.6) | copy-start | bytes 3076
  74.7 12.0 %copy-start.19 = (f32[512]{0:T(512)S(1)}, f32[512]{0:T(512)}, u32[]{:S(2)}) copy-start(f32[512]{0:T(512)} %param.7) | copy-start | bytes 6148
  201.4 2.2 copy-start.10
  206.9 13.0 %copy-start.2 = (f32[4,512,1024]{1,2,0:T(8,128)}, f32[4,512,1024]{1,2,0:T(8,128)S(1)}, u32[]{:S(2)}) copy-start(f32[4,512,1024]{1,2,0:T(8,128)S(1)} %constant_dynamic-update-slice_fusion) | copy-start | bytes 25165828
  224.4 2.7 copy-start.5
  224.4 4.0 copy-start.3
  231.1 9.2 %copy-start.13 = (f32[512,512]{0,1:T(8,128)S(1)}, f32[512,512]{0,1:T(8,128)}, u32[]{:S(2)}) copy-start(f32[512,512]{0,1:T(8,128)} %copy.26) | copy-start | bytes 3145732
  231.1 17.9 %slice-start = ((s8[8388608]{0:T(1024)(128)(4,1)}), s8[4194304]{0:T(1024)(128)(4,1)S(1)}, s32[]{:S(2)}) async-start(s8[8388608]{0:T(1024)(128)(4,1)} %bitcast.111), calls=%async_computation.5 | async-start | bytes 8388608
  240.3 8.7 %slice-start.1 = ((s8[8388608]{0:T(1024)(128)(4,1)}), s8[4194304]{0:T(1024)(128)(4,1)S(1)}, s32[]{:S(2)}) async-start(s8[8388608]{0:T(1024)(128)(4,1)} %bitcast.111), calls=%async_computation.6 | async-start | bytes 8388608
  240.3 8.7 %copy-start.11 = (f32[512,512]{0,1:T(8,128)S(1)}, f32[512,512]{0,1:T(8,128)}, u32[]{:S(2)}) copy-start(f32[512,512]{0,1:T(8,128)} %copy.27) | copy-start | bytes 3145732
  249.1 7.2 %copy-start.7 = (f32[512,512]{1,0:T(8,128)S(1)}, f32[512,512]{1,0:T(8,128)}, u32[]{:S(2)}) copy-start(f32[512,512]{1,0:T(8,128)} %fusion.14) | copy-start | bytes 3145732
  249.1 7.2 %copy-start.16 = (f32[512,512]{0,1:T(8,128)S(1)}, f32[512,512]{0,1:T(8,128)}, u32[]{:S(2)}) copy-start(f32[512,512]{0,1:T(8,128)} %copy.24) | copy-start | bytes 3145732
  267.2 226.8 %all-to-all-start.1 = ((f32[1,512,1024]{1,0,2:T(1,128)}), f32[1,512,1024]{1,0,2:T(1,128)S(1)}, u32[]{:S(2)}, u32[]{:S(2)}) async-start(f32[1,512,1024]{1,0,2:T(1,128)} %copy.28), calls=%async_computation.1 | async-start | bytes 4194304 | tf_op jit(solution)/shard_map/all_to_all | solution.py:78
  273.9 96.4 %all-reduce.5.cloned.1.call-start = ((), (), s32[]{:S(2)}) async-start(), calls=%async_computation.2 | async-start | bytes 2097152 | tf_op jit(solution)/shard_map/psum | solution.py:79
  274.2 4.5 copy-start.6
  274.2 4.5 copy-start.15
  278.7 2.5 copy-start.4
  278.7 2.5 copy-start.14
  281.2 2.5 copy-start.12
  287.3 204.4 %all-reduce.7.cloned.1.call-start = ((), (), s32[]{:S(2)}) async-start(), calls=%async_computation.3 | async-start | bytes 2097152 | tf_op jit(solution)/shard_map/psum | solution.py:79
  (3 other events, 3.9 us)
Sparse Core Ops, SparseCore 0:
  74.9 126.4 all-reduce.8
  287.4 82.8 all-reduce.4
  373.5 118.1 all-reduce.6
